TPU v7x, 32 devices: a whole 2x2x4 slice. The times are simulated.
32 devices in a mesh: stratum: 8 (over z, y), tm: 4 (over x, core).
Axes of the slice: x: 2, y: 2, z: 4, core: 2. Of those that a mesh axis runs over, the one named last changes fastest.
Arguments:
- row_factors: float32 [32768, 256], P(('stratum', 'tm')), may hold values from -0.75 to 0.75
- time_factors: float32 [32768, 256], P(('stratum', 'tm')), may hold values from -3 to 3
- values: bfloat16 [2, 32768, 1024], P(None, ('stratum', 'tm')), may hold values from -6 to 6
- tile_mask: int32 [2, 256, 8], P(None, ('stratum', 'tm')), may hold values from 0 to 1, as said below
- lags: int32 [4], replicated, may hold values from 1 to 64, as said below
- ar_weights: float32 [4], replicated, may hold values from -0.4 to 0.4
Outputs:
- rows_out: float32 [32768, 256], P(('stratum', 'tm'))
- time_out: float32 [32768, 256], P(('stratum', 'tm'))
Inputs may be any that keep to these rules, and one draw needn't show every extreme that they name: `tile_mask`: 0 or 1; in each sub-epoch each band of 128 series has its own chance of an observed tile, from an eighth to one. `lags`: distinct; the largest is exactly 64.
All inputs are finite; a program needn't handle non-finite values.
Results may differ from a plain program's by a relative error of at most 0.00082.
Values may be sent and summed in bfloat16 or wider, within the bound.
A program may use at most 64 MiB of HBM per device.

v0:
```python
import jax
import jax.numpy as jnp
from jax import lax
from jax.sharding import PartitionSpec as P

HALO = 64
LAGS = 4
TILE = 128


rate_rows = 0.005
rate_time = 0.02
ridge_rows = 16.0
ridge_time = 2.0
ridge_lags = 8.0


def padded(cells, sides, width):
    for axis, dim in sides:
        count = lax.axis_size(axis)
        head = lax.slice_in_dim(cells, 0, width, axis=dim)
        tail = lax.slice_in_dim(cells, cells.shape[dim] - width, cells.shape[dim], axis=dim)
        cells = jnp.concatenate(
            [
                lax.ppermute(tail, axis, [(i, (i + 1) % count) for i in range(count)]),
                cells,
                lax.ppermute(head, axis, [((i + 1) % count, i) for i in range(count)]),
            ],
            axis=dim,
        )
    return cells


def from_behind(value, axis, steps):
    count = lax.axis_size(axis)
    pairs = [(source, (source + steps) % count) for source in range(count)]
    return lax.ppermute(value, axis, pairs)


def block_step(rows, times, observed, marks):
    rows_low = rows.astype(jnp.bfloat16)
    times_low = times.astype(jnp.bfloat16)
    product = lax.dot_general(
        rows_low, times_low, (((1,), (1,)), ((), ())), preferred_element_type=jnp.float32
    )
    diff = observed.astype(jnp.float32) - product
    bands = marks.shape[0]
    columns = marks.shape[1]
    spread = diff.reshape(bands, TILE, columns, TILE) * marks.astype(jnp.float32)[:, None, :, None]
    masked = spread.reshape(diff.shape).astype(jnp.bfloat16)
    grad_rows = jnp.dot(masked, times_low, preferred_element_type=jnp.float32)
    grad_time = lax.dot_general(
        masked, rows_low, (((0,), (0,)), ((), ())), preferred_element_type=jnp.float32
    )
    return (rows + rate_rows * (grad_rows - ridge_rows * rows), grad_time)


def neighbour_rims(time_now):
    return padded(time_now, ((("stratum", "tm"), 0),), HALO)


def send_on(block):
    return from_behind(block, "stratum", 1)


def send_back(block):
    return from_behind(block, "stratum", -1)


def lag_terms(extended, current, block_len, total_time, lags, ar_weights):
    start = current * block_len
    positions = start - HALO + jnp.arange(block_len + 2 * HALO, dtype=jnp.int32)
    inside = (positions >= 0) & (positions < total_time)
    extended = jnp.where(inside[:, None], extended, 0.0)
    errors = extended[HALO:]
    for which in range(LAGS):
        begin = HALO - lags[which]
        errors = errors - ar_weights[which] * lax.dynamic_slice_in_dim(
            extended, begin, block_len + HALO, 0
        )
    later = positions[HALO:]
    errors = jnp.where((later < total_time)[:, None], errors, 0.0)
    lag_grad = errors[:block_len]
    for which in range(LAGS):
        begin = lags[which]
        lag_grad = lag_grad - ar_weights[which] * lax.dynamic_slice_in_dim(
            errors, begin, block_len, 0
        )
    return lag_grad


def body(row_factors, time_factors, values, tile_mask, lags, ar_weights):
    strata = lax.axis_size("stratum")
    groups = lax.axis_size("tm")
    blocks = strata * groups
    block_len = time_factors.shape[0]
    total_time = block_len * blocks
    stratum = lax.axis_index("stratum")
    group_idx = lax.axis_index("tm")
    home = stratum * groups + group_idx
    visited = (stratum - 1) % strata * groups + group_idx
    rows_now = row_factors
    time_now = time_factors
    extended = neighbour_rims(time_now)
    lag_grad = lag_terms(extended, home, block_len, total_time, lags, ar_weights)
    rows_now, grad_time = block_step(rows_now, time_now, values[0], tile_mask[0])
    time_now = time_now + rate_time * (grad_time - ridge_time * time_now - ridge_lags * lag_grad)
    time_now = send_on(time_now)
    extended = neighbour_rims(time_now)
    lag_grad = lag_terms(extended, visited, block_len, total_time, lags, ar_weights)
    rows_now, grad_time = block_step(rows_now, time_now, values[1], tile_mask[1])
    time_now = time_now + rate_time * (grad_time - ridge_time * time_now - ridge_lags * lag_grad)
    time_now = send_back(time_now)
    return (rows_now, time_now)


def solution(mesh):
    return jax.shard_map(
        body,
        mesh=mesh,
        in_specs=(
            P(("stratum", "tm"), None),
            P(("stratum", "tm"), None),
            P(None, ("stratum", "tm"), None),
            P(None, ("stratum", "tm"), None),
            P(),
            P(),
        ),
        out_specs=(P(("stratum", "tm"), None), P(("stratum", "tm"), None)),
        check_vma=False,
    )
```

profile of v0, /device:TPU:0, one launch (start us, length us, event | category | flops | bytes accessed | tf_op | source)
XLA Modules:
  0.0 104.3 jit_solution(5416766361759244460)
XLA Ops:
  0.6 0.9 fusion.40
  1.5 0.5 collective-permute-start
  2.0 6.0 %collective-permute-start.1 = (f32[64,256]{1,0:T(8,128)S(1)}, f32[64,256]{1,0:T(8,128)S(1)}, u32[]{:S(2)}, u32[]{:S(2)}) collective-permute-start(f32[64,256]{1,0:T(8,128)S(1)} %get-tuple-element.5), channel_id=1, source_target_pairs={{1,0},{2,1},{3,2},{4,3},{5,4},{6,5},{7,6},{8,7},{9,8},{10,9},{11,1... | collective-permute-start | bytes 196616 | tf_op jit(solution)/shard_map/ppermute | solution.py:27
  8.0 1.4 %fusion.42 = (s32[1]{0:T(128)}, s32[1]{0:T(128)}, s32[1]{0:T(128)}, s32[1]{0:T(128)}) fusion(s32[4]{0:T(128)} %param.10), kind=kLoop, calls=%fused_computation.61 | loop fusion | bytes 32 | tf_op jit(solution)/shard_map/slice | solution.py:77
  19.4 1.5 %fusion.41 = (f32[1]{0:T(128)}, f32[1]{0:T(128)}, f32[1]{0:T(128)}, f32[1]{0:T(128)}) fusion(f32[4]{0:T(128)} %param.11), kind=kLoop, calls=%fused_computation.60 | loop fusion | bytes 32 | tf_op jit(solution)/shard_map/slice | solution.py:78
  20.9 0.1 slice_compare_fusion.1
  21.0 0.7 convert_bitcast_fusion
  24.2 0.0 copy-start
  24.2 0.0 copy-start.1
  24.2 0.3 mul.144
  24.5 0.9 copy-done
  25.4 0.3 copy-done.1
  25.7 2.7 %fusion.1 = bf16[1024,1024]{1,0:T(8,128)(2,1)S(1)} fusion(f32[128,8,8,128]{3,2,1,0:T(8,128)S(1)} %bitcast.34, bf16[2,1024,1024]{2,1,0:T(8,128)(2,1)} %param.8, f32[1024,256]{1,0:T(8,128)S(1)} %copy-done, f32[1024,256]{1,0:T(8,128)S(1)} %copy-done.1), kind=kOutput, calls=%fused_computation.3 | convolution fusion | flops 541589504 | bytes 10485760 | tf_op jit(solution)/shard_map/dot_general | solution.py:43
  28.5 0.0 collective-permute-done
  28.5 0.0 collective-permute-done.1
  28.5 0.2 maximum_select_fusion
  28.7 3.2 %fusion.16 = f32[1088,256]{1,0:T(8,128)S(1)} fusion(f32[1152,256]{1,0:T(8,128)S(1)} %maximum_select_fusion, s32[]{:T(128)S(6)} %select_n.57, s32[]{:T(128)S(6)} %select_n.56, s32[]{:T(128)S(6)} %select_n.55, s32[]{:T(128)S(6)} %select_n.54, f32[]{:T(128)} %bitcast.9, f32[]{:T(128)} %bitcast.7, f32[]{:T(128)} %bitcast.5, f32[]{:T(128)} %bitcast.3, ...), kind=kLoop, calls=%fused_computation.27 | loop fusion | flops 2506752 | bytes 6685792 | tf_op jit(solution)/shard_map/jit(_where)/select_n | solution.py:82
  31.9 4.8 %fusion.6 = f32[1024,256]{1,0:T(8,128)} fusion(f32[1024,256]{1,0:T(8,128)S(1)} %copy-done, bf16[1024,1024]{1,0:T(8,128)(2,1)S(1)} %fusion.1, f32[1088,256]{1,0:T(8,128)S(1)} %fusion.16, s32[]{:T(128)S(6)} %select_n.62, s32[]{:T(128)S(6)} %select_n.61, s32[]{:T(128)S(6)} %select_n.60, s32[]{:T(128)S(6)} %select_n.59, f32[]{:T(128)} %bitcast.9, f32[]{:T(128)} %bitcast.7, ...), kind=kOutput, calls=%fused_computation.12 | convolution fusion | flops 540803072 | bytes 10485792 | tf_op jit(solution)/shard_map/dot_general | solution.py:52
  36.7 0.0 collective-permute-start.2
  36.7 0.1 slice_compare_fusion
  36.8 1.9 %fusion.8 = f32[1024,256]{1,0:T(8,128)S(1)} fusion(f32[1024,256]{1,0:T(8,128)} %param.6, bf16[1024,1024]{1,0:T(8,128)(2,1)S(1)} %fusion.1, f32[1024,256]{1,0:T(8,128)S(1)} %copy-done), kind=kOutput, calls=%fused_computation.15 | convolution fusion | flops 538181632 | bytes 5242880 | tf_op jit(solution)/shard_map/dot_general | solution.py:51
  38.7 22.8 %collective-permute-done.2 = f32[1024,256]{1,0:T(8,128)} collective-permute-done((f32[1024,256]{1,0:T(8,128)}, f32[1024,256]{1,0:T(8,128)}, u32[]{:S(2)}, u32[]{:S(2)}) %collective-permute-start.2) | collective-permute-done | bytes 1048608 | tf_op jit(solution)/shard_map/ppermute | solution.py:37
  61.5 0.9 fusion.39
  62.4 0.1 collective-permute-start.3
  62.5 5.3 %collective-permute-start.4 = (f32[64,256]{1,0:T(8,128)S(1)}, f32[64,256]{1,0:T(8,128)S(1)}, u32[]{:S(2)}, u32[]{:S(2)}) collective-permute-start(f32[64,256]{1,0:T(8,128)S(1)} %get-tuple-element.3), channel_id=1, source_target_pairs={{1,0},{2,1},{3,2},{4,3},{5,4},{6,5},{7,6},{8,7},{9,8},{10,9},{11,1... | collective-permute-start | bytes 196616 | tf_op jit(solution)/shard_map/ppermute | solution.py:27
  67.8 0.0 copy-start.2
  67.8 0.3 mul.170
  68.1 1.8 %copy-done.2 = bf16[2,1024,1024]{2,1,0:T(8,128)(2,1)S(1)} copy-done((bf16[2,1024,1024]{2,1,0:T(8,128)(2,1)S(1)}, bf16[2,1024,1024]{2,1,0:T(8,128)(2,1)}, u32[]{:S(2)}) %copy-start.2) | copy-done | bytes 4194328
  70.0 2.4 %fusion = bf16[1024,1024]{1,0:T(8,128)(2,1)S(1)} fusion(f32[128,8,8,128]{3,2,1,0:T(8,128)S(1)} %bitcast.35, bf16[2,1024,1024]{2,1,0:T(8,128)(2,1)S(1)} %copy-done.2, f32[1024,256]{1,0:T(8,128)} %collective-permute-done.2, f32[1024,256]{1,0:T(8,128)S(1)} %fusion.8), kind=kOutput, calls=%fused_computation.1 | convolution fusion | flops 541589504 | bytes 10485760 | tf_op jit(solution)/shard_map/dot_general | solution.py:43
  72.3 0.0 collective-permute-done.3
  72.3 0.0 collective-permute-done.4
  72.4 1.4 %maximum_select_fusion.1 = f32[1152,256]{1,0:T(8,128)S(1)} fusion(f32[64,256]{1,0:T(8,128)S(1)} %collective-permute-done.4, f32[1024,256]{1,0:T(8,128)} %collective-permute-done.2, f32[64,256]{1,0:T(8,128)S(1)} %collective-permute-done.3, pred[1152]{0:T(1024)(128)(4,1)S(1)} %compare_and_fusion), kind=kLoop, calls=%fused_computation.17 | loop fusion | flops 884736 | bytes 2360448 | tf_op jit(solution)/shard_map/jit(_where)/select_n | solution.py:74
  73.8 3.2 %fusion.12 = f32[1088,256]{1,0:T(8,128)S(1)} fusion(f32[1152,256]{1,0:T(8,128)S(1)} %maximum_select_fusion.1, s32[]{:T(128)S(6)} %select_n.57, s32[]{:T(128)S(6)} %select_n.56, s32[]{:T(128)S(6)} %select_n.55, s32[]{:T(128)S(6)} %select_n.54, f32[]{:T(128)} %bitcast.9, f32[]{:T(128)} %bitcast.7, f32[]{:T(128)} %bitcast.5, f32[]{:T(128)} %bitcast.3, ...), kind=kLoop, calls=%fused_computation.22 | loop fusion | flops 2506752 | bytes 6685792 | tf_op jit(solution)/shard_map/jit(_where)/select_n | solution.py:82
  77.0 5.1 %fusion.23 = f32[1024,256]{1,0:T(8,128)S(1)} fusion(f32[1024,256]{1,0:T(8,128)} %collective-permute-done.2, f32[1088,256]{1,0:T(8,128)S(1)} %fusion.12, s32[]{:T(128)S(6)} %select_n.62, s32[]{:T(128)S(6)} %select_n.61, s32[]{:T(128)S(6)} %select_n.60, s32[]{:T(128)S(6)} %select_n.59, f32[]{:T(128)} %bitcast.9, f32[]{:T(128)} %bitcast.7, f32[]{:T(128)} %bitcast.5, ...), kind=kOutput, calls=%fused_computation.35 | convolution fusion | flops 540803072 | bytes 10485792 | tf_op jit(solution)/shard_map/dot_general | solution.py:52
  82.1 0.1 collective-permute-start.5
  82.1 2.9 %fusion.3 = f32[1024,256]{1,0:T(8,128)} fusion(f32[1024,256]{1,0:T(8,128)S(1)} %fusion.8, bf16[1024,1024]{1,0:T(8,128)(2,1)S(1)} %fusion, f32[1024,256]{1,0:T(8,128)} %collective-permute-done.2), kind=kOutput, calls=%fused_computation.8 | convolution fusion | flops 538181632 | bytes 5242880 | tf_op jit(solution)/shard_map/dot_general | solution.py:51
  85.0 18.3 %collective-permute-done.5 = f32[1024,256]{1,0:T(8,128)S(1)} collective-permute-done((f32[1024,256]{1,0:T(8,128)S(1)}, f32[1024,256]{1,0:T(8,128)S(1)}, u32[]{:S(2)}, u32[]{:S(2)}) %collective-permute-start.5) | collective-permute-done | bytes 1048608 | tf_op jit(solution)/shard_map/ppermute | solution.py:37
  103.3 1.0 copy.13
  (4 shorter events, 0.0 us)
Async XLA Ops:
  1.5 26.9 %collective-permute-start = (f32[64,256]{1,0:T(8,128)S(1)}, f32[64,256]{1,0:T(8,128)S(1)}, u32[]{:S(2)}, u32[]{:S(2)}) collective-permute-start(f32[64,256]{1,0:T(8,128)S(1)} %get-tuple-element.4), channel_id=1, source_target_pairs={{0,1},{1,2},{2,3},{3,4},{4,5},{5,6},{6,7},{7,8},{8,9},{9,10},{10,1... | collective-permute-start | bytes 196616 | tf_op jit(solution)/shard_map/ppermute | solution.py:25
  2.0 26.4 %collective-permute-start.1 = (f32[64,256]{1,0:T(8,128)S(1)}, f32[64,256]{1,0:T(8,128)S(1)}, u32[]{:S(2)}, u32[]{:S(2)}) collective-permute-start(f32[64,256]{1,0:T(8,128)S(1)} %get-tuple-element.5), channel_id=1, source_target_pairs={{1,0},{2,1},{3,2},{4,3},{5,4},{6,5},{7,6},{8,7},{9,8},{10,9},{11,1... | collective-permute-start | bytes 196616 | tf_op jit(solution)/shard_map/ppermute | solution.py:27
  24.2 1.2 %copy-start = (f32[1024,256]{1,0:T(8,128)S(1)}, f32[1024,256]{1,0:T(8,128)}, u32[]{:S(2)}) copy-start(f32[1024,256]{1,0:T(8,128)} %param.7) | copy-start | bytes 3145732
  24.2 1.5 %copy-start.1 = (f32[1024,256]{1,0:T(8,128)S(1)}, f32[1024,256]{1,0:T(8,128)}, u32[]{:S(2)}) copy-start(f32[1024,256]{1,0:T(8,128)} %param.6) | copy-start | bytes 3145732
  36.7 24.8 %collective-permute-start.2 = (f32[1024,256]{1,0:T(8,128)}, f32[1024,256]{1,0:T(8,128)}, u32[]{:S(2)}, u32[]{:S(2)}) collective-permute-start(f32[1024,256]{1,0:T(8,128)} %fusion.6), channel_id=1, source_target_pairs={{0,4},{4,8},{8,12},{12,16},{16,20},{20,24},{24,28},{28,0},{1,5},{5... | collective-permute-start | bytes 3145736 | tf_op jit(solution)/shard_map/ppermute | solution.py:37
  62.4 9.9 %collective-permute-start.3 = (f32[64,256]{1,0:T(8,128)S(1)}, f32[64,256]{1,0:T(8,128)S(1)}, u32[]{:S(2)}, u32[]{:S(2)}) collective-permute-start(f32[64,256]{1,0:T(8,128)S(1)} %get-tuple-element.2), channel_id=1, source_target_pairs={{0,1},{1,2},{2,3},{3,4},{4,5},{5,6},{6,7},{7,8},{8,9},{9,10},{10,1... | collective-permute-start | bytes 196616 | tf_op jit(solution)/shard_map/ppermute | solution.py:25
  62.5 9.9 %collective-permute-start.4 = (f32[64,256]{1,0:T(8,128)S(1)}, f32[64,256]{1,0:T(8,128)S(1)}, u32[]{:S(2)}, u32[]{:S(2)}) collective-permute-start(f32[64,256]{1,0:T(8,128)S(1)} %get-tuple-element.3), channel_id=1, source_target_pairs={{1,0},{2,1},{3,2},{4,3},{5,4},{6,5},{7,6},{8,7},{9,8},{10,9},{11,1... | collective-permute-start | bytes 196616 | tf_op jit(solution)/shard_map/ppermute | solution.py:27
  67.8 2.2 %copy-start.2 = (bf16[2,1024,1024]{2,1,0:T(8,128)(2,1)S(1)}, bf16[2,1024,1024]{2,1,0:T(8,128)(2,1)}, u32[]{:S(2)}) copy-start(bf16[2,1024,1024]{2,1,0:T(8,128)(2,1)} %param.8) | copy-start | bytes 12582916
  82.1 21.3 %collective-permute-start.5 = (f32[1024,256]{1,0:T(8,128)S(1)}, f32[1024,256]{1,0:T(8,128)S(1)}, u32[]{:S(2)}, u32[]{:S(2)}) collective-permute-start(f32[1024,256]{1,0:T(8,128)S(1)} %fusion.23), channel_id=1, source_target_pairs={{0,28},{4,0},{8,4},{12,8},{16,12},{20,16},{24,20},{28,24},{1,29},{... | collective-permute-start | bytes 3145736 | tf_op jit(solution)/shard_map/ppermute | solution.py:37
where the time goes:
time: 105 us; the launch traced here: 104 us
  waiting for transfers between devices  41.1 us (39%)
  matrix products  19.8 us (19%)
  between operations  13.3 us (13%)
  starting transfers between devices  11.9 us (11%)
  local copies, waits for them, and re-layouts  9.33 us (9%)
  other arithmetic  8.86 us (8%)
    ppermute x2, waiting for transfers between devices, from_behind(): return lax.ppermute(value, axis, pairs)  41.1 us
    ppermute x2, starting transfers between devices, padded(): lax.ppermute(head, axis, [((i + 1) % count, i) for i in range(count)])  11.3 us
    dot_general x2, matrix products, block_step(): lax.dot_general(masked, rows_low, (((0,), (0,)), ((), ())), preferred_ele...  9.9 us
    select_n x2, other arithmetic, lag_terms(): errors = jnp.where((later < total_time)[:, None], errors, 0.0)  6.31 us
    dot_general x2, matrix products, block_step(): lax.dot_general(rows_low, times_low, (((1,), (1,)), ((), ())), preferred_...  5.09 us
    dot_general x2, matrix products, block_step(): grad_rows = jnp.dot(masked, times_low, preferred_element_type=jnp.float32)  4.85 us
    unnamed x7, local copies, waits for them, and re-layouts  4 us
  transfers between devices with their start and end apart: 6, of which 2 were waited for; matrix products, arithmetic and copies ran while one was open for 14% of the time, Pallas kernels for 0%

commit v1 on v0

v1 whole, which is shorter than its diff:
```python
import functools

import jax
import jax.numpy as jnp
from jax import lax
from jax.experimental import pallas as pl
from jax.experimental.pallas import tpu as pltpu
from jax.sharding import PartitionSpec as P

HALO = 64
LAGS = 4
TILE = 128
CHUNK = 256
BAND = 128
PAD = 16
TOP = 32000.0
LOG2_E = 1.4426950408889634

rate_rows = 0.005
rate_time = 0.02
ridge_rows = 16.0
ridge_time = 2.0
ridge_lags = 8.0

MESH = pl.DeviceIdType.MESH
NT = (((1,), (1,)), ((), ()))


def chunk_order(count):
    inner = list(range(1, count - 1))
    return inner + [0, count - 1] if count > 1 else [0]


def kernel(strata, groups, lags, weights, mask, f_hbm, x_hbm, v_hbm, f_out, x_out,
           f, x, v0, v1, r, x1, fb, fbt, xh0, xl0, xh1, xl1, xr, gs, gr, lo0, hi0, lo1, hi1, coef,
           load_sem, out_sem, send_sem, recv_sem, hsend_sem, hrecv_sem):
    block_len = x.shape[0]
    rows = f.shape[0]
    count = block_len // CHUNK
    order = chunk_order(count)
    last = block_len - HALO
    blocks = strata * groups
    s = lax.axis_index("stratum")
    g = lax.axis_index("tm")
    c = s * groups + g
    cr = lax.rem(c + 1, blocks)
    cl = lax.rem(c + blocks - 1, blocks)
    right = (cr // groups, lax.rem(cr, groups))
    left = (cl // groups, lax.rem(cl, groups))
    nxt = (lax.rem(s + 1, strata), g)
    prv = (lax.rem(s + strata - 1, strata), g)

    def cols(j):
        return pl.ds(j * CHUNK, CHUNK)

    def inner(j):
        return pl.ds(HALO + j * CHUNK, CHUNK)

    load_x = pltpu.make_async_copy(x_hbm, x, load_sem.at[0])
    load_f = pltpu.make_async_copy(f_hbm, f, load_sem.at[1])
    load_v1 = pltpu.make_async_copy(v_hbm.at[1], v1, load_sem.at[2])
    load_v0 = {
        j: pltpu.make_async_copy(v_hbm.at[0, :, cols(j)], v0.at[:, cols(j)], load_sem.at[3 + j])
        for j in order
    }
    load_x.start()
    load_f.start()
    for j in order:
        load_v0[j].start()
    load_v1.start()

    barrier = pltpu.get_barrier_semaphore()
    for peer in (left, right, nxt, prv):
        pl.semaphore_signal(barrier, inc=1, device_id=peer, device_id_type=MESH)
    pl.semaphore_wait(barrier, 4)

    def rims(first, final, lo, hi, at):
        to_right = pltpu.make_async_remote_copy(
            src_ref=final, dst_ref=lo, send_sem=hsend_sem.at[at],
            recv_sem=hrecv_sem.at[at], device_id=right, device_id_type=MESH)
        to_left = pltpu.make_async_remote_copy(
            src_ref=first, dst_ref=hi, send_sem=hsend_sem.at[at + 1],
            recv_sem=hrecv_sem.at[at + 1], device_id=left, device_id_type=MESH)
        return to_right, to_left

    rim0_r, rim0_l = rims(x_hbm.at[pl.ds(0, HALO)], x_hbm.at[pl.ds(last, HALO)], lo0, hi0, 0)
    rim1_r, rim1_l = rims(x1.at[pl.ds(0, HALO)], x1.at[pl.ds(last, HALO)], lo1, hi1, 2)
    rim0_r.start()
    rim0_l.start()
    forth = {
        j: pltpu.make_async_remote_copy(
            src_ref=xh1.at[inner(j)], dst_ref=xr.at[cols(j)], send_sem=send_sem.at[j],
            recv_sem=recv_sem.at[j], device_id=nxt, device_id_type=MESH)
        for j in order
    }
    back = {
        j: pltpu.make_async_remote_copy(
            src_ref=gs.at[j], dst_ref=gr.at[j], send_sem=send_sem.at[count + j],
            recv_sem=recv_sem.at[count + j], device_id=prv, device_id_type=MESH)
        for j in order
    }

    lag = [lags[which] for which in range(LAGS)]
    weight = [weights[which] for which in range(LAGS)]
    step = lax.broadcasted_iota(jnp.int32, (BAND, BAND + 2 * HALO), 0)
    offset = lax.broadcasted_iota(jnp.int32, (BAND, BAND + 2 * HALO), 1) - HALO - step
    behind = jnp.where(offset == 0, 1.0, 0.0)
    for which in range(LAGS):
        behind = behind - jnp.where(offset == -lag[which], weight[which], 0.0)
    usual, final = behind, behind
    for which in range(LAGS):
        ahead = jnp.where(offset == lag[which], weight[which], 0.0)
        for other in range(LAGS):
            ahead = ahead - jnp.where(
                offset == lag[which] - lag[other], weight[which] * weight[other], 0.0)
        usual = usual - ahead
        held = (step + lag[which] < BAND) | (c < blocks - 1)
        final = final - jnp.where(held, ahead, 0.0)
    for at, matrix in enumerate((usual, final)):
        high = matrix.astype(jnp.bfloat16)
        coef[2 * at] = high
        coef[2 * at + 1] = (matrix - high.astype(jnp.float32)).astype(jnp.bfloat16)

    def split(value, high_ref, low_ref, at, size):
        high = value.astype(jnp.bfloat16)
        high_ref[pl.ds(at, size), :] = high
        low_ref[pl.ds(at, size), :] = (value - high.astype(jnp.float32)).astype(jnp.bfloat16)

    def rim_low(lo, high_ref, low_ref):
        split(jnp.where(c > 0, lo[...], 0.0), high_ref, low_ref, 0, HALO)

    def rim_high(hi, high_ref, low_ref):
        split(hi[...], high_ref, low_ref, HALO + block_len, HALO)

    def lag_grad(high_ref, low_ref, j):
        bands = []
        for band in range(j * CHUNK // BAND, (j + 1) * CHUNK // BAND):
            near = pl.ds(band * BAND, BAND + 2 * HALO)
            at = 2 if band == block_len // BAND - 1 else 0
            high = high_ref[near, :]
            bands.append(
                jnp.dot(coef[at], high, preferred_element_type=jnp.float32)
                + jnp.dot(coef[at], low_ref[near, :], preferred_element_type=jnp.float32)
                + jnp.dot(coef[at + 1], high, preferred_element_type=jnp.float32))
        return jnp.concatenate(bands, axis=0)

    def chunk_grad(k, j, times, v):
        for band in range(rows // CHUNK):
            product = lax.dot_general(
                fb[pl.ds(band * CHUNK, CHUNK), :], times, NT, preferred_element_type=jnp.float32)
            for i in range(CHUNK // TILE):
                for l in range(CHUNK // TILE):
                    mark = mask[k, band * (CHUNK // TILE) + i, j * (CHUNK // TILE) + l].astype(jnp.float32)
                    here = (pl.ds(band * CHUNK + i * TILE, TILE), pl.ds(j * CHUNK + l * TILE, TILE))
                    tile = product[i * TILE:(i + 1) * TILE, l * TILE:(l + 1) * TILE]
                    r[here] = ((v[here].astype(jnp.float32) - tile) * mark).astype(jnp.bfloat16)
        grad = jnp.dot(fbt[...], r[:, cols(j)], preferred_element_type=jnp.float32)
        return grad.T

    def rows_step(times, base):
        for band in range(rows // CHUNK):
            here = pl.ds(band * CHUNK, CHUNK)
            grad = jnp.dot(
                r[here, :], times[pl.ds(base, block_len), :], preferred_element_type=jnp.float32)
            f[here, :] = f[here, :] + rate_rows * (grad - ridge_rows * f[here, :])

    def round_rows():
        for band in range(rows // CHUNK):
            here = pl.ds(band * CHUNK, CHUNK)
            low = f[here, :].astype(jnp.bfloat16)
            fb[here, :] = low
            fbt[:, here] = low.T

    def pack(grad, j):
        top = jnp.maximum(jnp.max(jnp.abs(grad), axis=0, keepdims=True), 1e-30)
        power = jnp.broadcast_to(jnp.ceil(jnp.log(top) * LOG2_E), (PAD, grad.shape[1]))
        per_unit = TOP * jnp.exp2(-power[:1, :])
        gs[j, pl.ds(0, CHUNK), :] = jnp.floor(grad * per_unit + 0.5).astype(jnp.int32).astype(jnp.int16)
        gs[j, pl.ds(CHUNK, PAD), :] = power.astype(jnp.int32).astype(jnp.int16)

    def unpack(j):
        power = gr[j, pl.ds(CHUNK, PAD), :].astype(jnp.int32).astype(jnp.float32)
        unit = (1.0 / TOP) * jnp.exp2(power[:1, :])
        return gr[j, pl.ds(0, CHUNK), :].astype(jnp.int32).astype(jnp.float32) * unit

    def ridge_step(now, high_ref, low_ref, j):
        return now - rate_time * (ridge_time * now + ridge_lags * lag_grad(high_ref, low_ref, j))

    load_f.wait()
    round_rows()
    load_x.wait()
    for j in range(count):
        split(x[cols(j), :], xh0, xl0, HALO + j * CHUNK, CHUNK)
    for j in order:
        load_v0[j].wait()
        grad = chunk_grad(0, j, xh0[inner(j), :], v0)
        if j == 0:
            rim0_r.wait_recv()
            rim_low(lo0, xh0, xl0)
        if j == count - 1:
            rim0_l.wait_recv()
            rim_high(hi0, xh0, xl0)
        now = ridge_step(x[cols(j), :], xh0, xl0, j) + rate_time * grad
        x1[cols(j), :] = now
        split(now, xh1, xl1, HALO + j * CHUNK, CHUNK)
        forth[j].start()
    rim1_r.start()
    rim1_l.start()
    rows_step(xh0, HALO)
    round_rows()

    load_v1.wait()
    for j in order:
        forth[j].wait_recv()
        grad = chunk_grad(1, j, xr[cols(j), :], v1)
        pack(grad, j)
        back[j].start()
        if j == 0:
            rim1_r.wait_recv()
            rim_low(lo1, xh1, xl1)
        if j == count - 1:
            rim1_l.wait_recv()
            rim_high(hi1, xh1, xl1)
        x[cols(j), :] = ridge_step(x1[cols(j), :], xh1, xl1, j)
    rows_step(xr, 0)
    store_f = pltpu.make_async_copy(f, f_out, out_sem.at[0])
    store_f.start()

    stores = []
    for j in order:
        back[j].wait_recv()
        x[cols(j), :] = x[cols(j), :] + rate_time * unpack(j)
        store = pltpu.make_async_copy(x.at[cols(j)], x_out.at[cols(j)], out_sem.at[1 + j])
        store.start()
        stores.append(store)
    for j in order:
        forth[j].wait_send()
        back[j].wait_send()
    for rim in (rim0_r, rim0_l, rim1_r, rim1_l):
        rim.wait_send()
    store_f.wait()
    for store in stores:
        store.wait()


def body(row_factors, time_factors, values, tile_mask, lags, ar_weights):
    strata = lax.axis_size("stratum")
    groups = lax.axis_size("tm")
    block_len, rank = time_factors.shape
    rows = row_factors.shape[0]
    count = block_len // CHUNK
    f32, bf16 = jnp.float32, jnp.bfloat16
    smem = pl.BlockSpec(memory_space=pltpu.SMEM)
    hbm = pl.BlockSpec(memory_space=pl.ANY)
    return tuple(pl.pallas_call(
        functools.partial(kernel, strata, groups),
        out_shape=(
            jax.ShapeDtypeStruct((rows, rank), f32),
            jax.ShapeDtypeStruct((block_len, rank), f32),
        ),
        in_specs=[smem, smem, smem, hbm, hbm, hbm],
        out_specs=(hbm, hbm),
        scratch_shapes=[
            pltpu.VMEM((rows, rank), f32),
            pltpu.VMEM((block_len, rank), f32),
            pltpu.VMEM((rows, block_len), bf16),
            pltpu.VMEM((rows, block_len), bf16),
            pltpu.VMEM((rows, block_len), bf16),
            pltpu.VMEM((block_len, rank), f32),
            pltpu.VMEM((rows, rank), bf16),
            pltpu.VMEM((rank, rows), bf16),
            pltpu.VMEM((block_len + 2 * HALO, rank), bf16),
            pltpu.VMEM((block_len + 2 * HALO, rank), bf16),
            pltpu.VMEM((block_len + 2 * HALO, rank), bf16),
            pltpu.VMEM((block_len + 2 * HALO, rank), bf16),
            pltpu.VMEM((block_len, rank), bf16),
            pltpu.VMEM((count, CHUNK + PAD, rank), jnp.int16),
            pltpu.VMEM((count, CHUNK + PAD, rank), jnp.int16),
            pltpu.VMEM((HALO, rank), f32),
            pltpu.VMEM((HALO, rank), f32),
            pltpu.VMEM((HALO, rank), f32),
            pltpu.VMEM((HALO, rank), f32),
            pltpu.VMEM((4, BAND, BAND + 2 * HALO), bf16),
            pltpu.SemaphoreType.DMA((3 + count,)),
            pltpu.SemaphoreType.DMA((1 + count,)),
            pltpu.SemaphoreType.DMA((2 * count,)),
            pltpu.SemaphoreType.DMA((2 * count,)),
            pltpu.SemaphoreType.DMA((4,)),
            pltpu.SemaphoreType.DMA((4,)),
        ],
        compiler_params=pltpu.CompilerParams(
            collective_id=0, has_side_effects=True, vmem_limit_bytes=48 * 2**20),
    )(lags, ar_weights, tile_mask, row_factors, time_factors, values))


def solution(mesh):
    return jax.shard_map(
        body,
        mesh=mesh,
        in_specs=(
            P(("stratum", "tm"), None),
            P(("stratum", "tm"), None),
            P(None, ("stratum", "tm"), None),
            P(None, ("stratum", "tm"), None),
            P(),
            P(),
        ),
        out_specs=(P(("stratum", "tm"), None), P(("stratum", "tm"), None)),
        check_vma=False,
    )
```

time: 105 us -> 47.5 us (0.45)
  waiting for transfers between devices: 41.1 us -> 0 us
  Pallas kernels: 0 us -> 40.2 us
  matrix products: 19.8 us -> 0 us
  between operations: 13.3 us -> 0.65 us
  starting transfers between devices: 11.9 us -> 0 us
  other arithmetic: 8.86 us -> 0 us
  local copies, waits for them, and re-layouts: 9.33 us -> 6.39 us
    ppermute x6 -> x0, waiting for transfers between devices: 41.1 us -> none  [the longest x2 41.1 us: from_behind(): return lax.ppermute(value, axis, pairs)]
    pallas_call x0 -> x1, Pallas kernels: none -> 40.2 us  [body(): pl.pallas_call(functools.partial(kernel, strata, groups), out_shape=(jax....]
    dot_general x6 -> x0, matrix products: 19.8 us -> none  [the longest x2 9.9 us: block_step(): lax.dot_general(masked, rows_low, (((0,), (0,)), ((), ())), preferred_ele...]
    ppermute x6 -> x0, starting transfers between devices: 11.9 us -> none  [the longest x2 11.3 us: padded(): lax.ppermute(head, axis, [((i + 1) % count, i) for i in range(count)])]
    select_n x4 -> x0, other arithmetic: 7.97 us -> none  [the longest x2 6.31 us: lag_terms(): errors = jnp.where((later < total_time)[:, None], errors, 0.0)]
    slice x4 -> x0, local copies, waits for them, and re-layouts: 4.66 us -> none  [the longest x2 1.77 us: padded(): lax.slice_in_dim(cells, cells.shape[dim] - width, cells.shape[dim], axis=...]
    unnamed x7 -> x12, local copies, waits for them, and re-layouts: 4 us -> 6.39 us
  transfers between devices with their start and end apart: 6 -> 0, of which waited for: 2 -> 0; matrix products, arithmetic and copies ran while one was open for 14% -> 0% of each run, Pallas kernels for 0% -> 0%
where the time goes in v1:
time: 47.5 us; the launch traced here: 47.3 us
  Pallas kernels  40.2 us (85%)
  local copies, waits for them, and re-layouts  6.39 us (13%)
  between operations  0.65 us (1%)
    pallas_call x1, Pallas kernels, body(): pl.pallas_call(functools.partial(kernel, strata, groups), out_shape=(jax....  40.2 us
    unnamed x12, local copies, waits for them, and re-layouts  6.39 us

profile of v1, /device:TPU:0, one launch (start us, length us, event | category | flops | bytes accessed | tf_op | source)
XLA Modules:
  0.0 47.3 jit_solution(664085632956534362)
XLA Ops:
  0.6 0.0 copy-start
  0.6 1.2 %copy-done = f32[1024,256]{1,0:T(8,128)S(1)} copy-done((f32[1024,256]{1,0:T(8,128)S(1)}, f32[1024,256]{1,0:T(8,128)}, u32[]{:S(2)}) %copy-start) | copy-done | bytes 1048600
  1.9 0.0 copy-start.1
  1.9 1.2 %copy-done.1 = f32[1024,256]{1,0:T(8,128)S(1)} copy-done((f32[1024,256]{1,0:T(8,128)S(1)}, f32[1024,256]{1,0:T(8,128)}, u32[]{:S(2)}) %copy-start.1) | copy-done | bytes 1048600
  3.1 0.0 copy-start.2
  3.1 0.7 %copy-done.2 = s32[2,8,8]{2,1,0:T(8,128)S(1)} copy-done((s32[2,8,8]{2,1,0:T(8,128)S(1)}, s32[2,8,8]{2,1,0:T(8,128)}, u32[]{:S(2)}) %copy-start.2) | copy-done | bytes 536
  3.8 0.0 copy-start.3
  3.8 0.7 %copy-done.3 = s32[4]{0:T(128)S(1)} copy-done((s32[4]{0:T(128)S(1)}, s32[4]{0:T(128)}, u32[]{:S(2)}) %copy-start.3) | copy-done | bytes 40
  4.4 0.0 copy-start.4
  4.4 0.7 %copy-done.4 = f32[4]{0:T(128)S(1)} copy-done((f32[4]{0:T(128)S(1)}, f32[4]{0:T(128)}, u32[]{:S(2)}) %copy-start.4) | copy-done | bytes 40
  5.1 40.2 %shard_map.77 = (f32[1024,256]{1,0:T(8,128)S(1)}, f32[1024,256]{1,0:T(8,128)S(1)}) custom-call(s32[4]{0:T(128)S(1)} %copy-done.3, f32[4]{0:T(128)S(1)} %copy-done.4, s32[2,8,8]{2,1,0:T(8,128)S(1)} %copy-done.2, f32[1024,256]{1,0:T(8,128)S(1)} %copy-done, f32[1024,256]{1,0:T(8,128)S(1)} %copy-done.1, bf16[2,1024,1024]{2,1,0:T(8,128)(2,1)} %v_hbm.1), custom_call_target="tpu_custom_call" | custom-call | tf_op jit(solution)/shard_map/pallas_call | solution.py:255
  45.3 1.0 %copy.10 = f32[1024,256]{1,0:T(8,128)} copy(f32[1024,256]{1,0:T(8,128)S(1)} %get-tuple-element.4) | data formatting | bytes 2097152
  46.3 1.0 %copy.11 = f32[1024,256]{1,0:T(8,128)} copy(f32[1024,256]{1,0:T(8,128)S(1)} %get-tuple-element.5) | data formatting | bytes 2097152
Async XLA Ops:
  0.6 1.2 %copy-start = (f32[1024,256]{1,0:T(8,128)S(1)}, f32[1024,256]{1,0:T(8,128)}, u32[]{:S(2)}) copy-start(f32[1024,256]{1,0:T(8,128)} %f_hbm.1) | copy-start | bytes 3145732
  1.9 1.2 %copy-start.1 = (f32[1024,256]{1,0:T(8,128)S(1)}, f32[1024,256]{1,0:T(8,128)}, u32[]{:S(2)}) copy-start(f32[1024,256]{1,0:T(8,128)} %x_hbm.1) | copy-start | bytes 3145732
  3.1 0.7 %copy-start.2 = (s32[2,8,8]{2,1,0:T(8,128)S(1)}, s32[2,8,8]{2,1,0:T(8,128)}, u32[]{:S(2)}) copy-start(s32[2,8,8]{2,1,0:T(8,128)} %mask.1) | copy-start | bytes 1540
  3.8 0.7 %copy-start.3 = (s32[4]{0:T(128)S(1)}, s32[4]{0:T(128)}, u32[]{:S(2)}) copy-start(s32[4]{0:T(128)} %lags.1) | copy-start | bytes 52
  4.4 0.7 %copy-start.4 = (f32[4]{0:T(128)S(1)}, f32[4]{0:T(128)}, u32[]{:S(2)}) copy-start(f32[4]{0:T(128)} %weights.1) | copy-start | bytes 52

commit v2 on v1

--- a/solution.py
+++ b/solution.py
@@ -31,8 +31,8 @@
     return inner + [0, count - 1] if count > 1 else [0]
 
 
-def kernel(strata, groups, lags, weights, mask, f_hbm, x_hbm, v_hbm, f_out, x_out,
-           f, x, v0, v1, r, x1, fb, fbt, xh0, xl0, xh1, xl1, xr, gs, gr, lo0, hi0, lo1, hi1, coef,
+def kernel(strata, groups, lags_hbm, weights_hbm, mask_hbm, f_hbm, x_hbm, v_hbm, f_out, x_out,
+           f, x, v0, v1, r, x1, fb, fbt, xh0, xl0, xh1, xl1, xr, gs, gr, lo0, hi0, coef, lags, weights, mask,
            load_sem, out_sem, send_sem, recv_sem, hsend_sem, hrecv_sem):
     block_len = x.shape[0]
     rows = f.shape[0]
@@ -63,28 +63,31 @@
         j: pltpu.make_async_copy(v_hbm.at[0, :, cols(j)], v0.at[:, cols(j)], load_sem.at[3 + j])
         for j in order
     }
+    smalls = [
+        pltpu.make_async_copy(source, here, load_sem.at[3 + count + at])
+        for at, (source, here) in enumerate(((lags_hbm, lags), (weights_hbm, weights), (mask_hbm, mask)))
+    ]
+    for small in smalls:
+        small.start()
     load_x.start()
     load_f.start()
     for j in order:
         load_v0[j].start()
-    load_v1.start()
 
     barrier = pltpu.get_barrier_semaphore()
     for peer in (left, right, nxt, prv):
         pl.semaphore_signal(barrier, inc=1, device_id=peer, device_id_type=MESH)
     pl.semaphore_wait(barrier, 4)
 
-    def rims(first, final, lo, hi, at):
-        to_right = pltpu.make_async_remote_copy(
-            src_ref=final, dst_ref=lo, send_sem=hsend_sem.at[at],
-            recv_sem=hrecv_sem.at[at], device_id=right, device_id_type=MESH)
-        to_left = pltpu.make_async_remote_copy(
-            src_ref=first, dst_ref=hi, send_sem=hsend_sem.at[at + 1],
-            recv_sem=hrecv_sem.at[at + 1], device_id=left, device_id_type=MESH)
-        return to_right, to_left
-
-    rim0_r, rim0_l = rims(x_hbm.at[pl.ds(0, HALO)], x_hbm.at[pl.ds(last, HALO)], lo0, hi0, 0)
-    rim1_r, rim1_l = rims(x1.at[pl.ds(0, HALO)], x1.at[pl.ds(last, HALO)], lo1, hi1, 2)
+    def rim(source, target, at, peer):
+        return pltpu.make_async_remote_copy(
+            src_ref=source, dst_ref=target, send_sem=hsend_sem.at[at],
+            recv_sem=hrecv_sem.at[at], device_id=peer, device_id_type=MESH)
+
+    rim0_r = rim(x_hbm.at[pl.ds(last, HALO)], lo0, 0, right)
+    rim0_l = rim(x_hbm.at[pl.ds(0, HALO)], hi0, 1, left)
+    rim1_r = rim(xh1.at[pl.ds(block_len, HALO)], xh1.at[pl.ds(0, HALO)], 2, right)
+    rim1_l = rim(xh1.at[pl.ds(HALO, HALO)], xh1.at[pl.ds(HALO + block_len, HALO)], 3, left)
     rim0_r.start()
     rim0_l.start()
     forth = {
@@ -100,6 +103,8 @@
         for j in order
     }
 
+    for small in smalls:
+        small.wait()
     lag = [lags[which] for which in range(LAGS)]
     weight = [weights[which] for which in range(LAGS)]
     step = lax.broadcasted_iota(jnp.int32, (BAND, BAND + 2 * HALO), 0)
@@ -126,12 +131,6 @@
         high_ref[pl.ds(at, size), :] = high
         low_ref[pl.ds(at, size), :] = (value - high.astype(jnp.float32)).astype(jnp.bfloat16)
 
-    def rim_low(lo, high_ref, low_ref):
-        split(jnp.where(c > 0, lo[...], 0.0), high_ref, low_ref, 0, HALO)
-
-    def rim_high(hi, high_ref, low_ref):
-        split(hi[...], high_ref, low_ref, HALO + block_len, HALO)
-
     def lag_grad(high_ref, low_ref, j):
         bands = []
         for band in range(j * CHUNK // BAND, (j + 1) * CHUNK // BAND):
@@ -196,14 +195,16 @@
         grad = chunk_grad(0, j, xh0[inner(j), :], v0)
         if j == 0:
             rim0_r.wait_recv()
-            rim_low(lo0, xh0, xl0)
+            split(jnp.where(c > 0, lo0[...], 0.0), xh0, xl0, 0, HALO)
         if j == count - 1:
             rim0_l.wait_recv()
-            rim_high(hi0, xh0, xl0)
+            split(hi0[...], xh0, xl0, HALO + block_len, HALO)
         now = ridge_step(x[cols(j), :], xh0, xl0, j) + rate_time * grad
         x1[cols(j), :] = now
         split(now, xh1, xl1, HALO + j * CHUNK, CHUNK)
         forth[j].start()
+        if j == order[0]:
+            load_v1.start()
     rim1_r.start()
     rim1_l.start()
     rows_step(xh0, HALO)
@@ -217,10 +218,12 @@
         back[j].start()
         if j == 0:
             rim1_r.wait_recv()
-            rim_low(lo1, xh1, xl1)
+            head = xh1[pl.ds(0, HALO), :]
+            xh1[pl.ds(0, HALO), :] = jnp.where(c > 0, head, jnp.zeros_like(head))
+            xl1[pl.ds(0, HALO), :] = jnp.zeros_like(head)
         if j == count - 1:
             rim1_l.wait_recv()
-            rim_high(hi1, xh1, xl1)
+            xl1[pl.ds(HALO + block_len, HALO), :] = jnp.zeros((HALO, x.shape[1]), jnp.bfloat16)
         x[cols(j), :] = ridge_step(x1[cols(j), :], xh1, xl1, j)
     rows_step(xr, 0)
     store_f = pltpu.make_async_copy(f, f_out, out_sem.at[0])
@@ -236,8 +239,8 @@
     for j in order:
         forth[j].wait_send()
         back[j].wait_send()
-    for rim in (rim0_r, rim0_l, rim1_r, rim1_l):
-        rim.wait_send()
+    for side in (rim0_r, rim0_l, rim1_r, rim1_l):
+        side.wait_send()
     store_f.wait()
     for store in stores:
         store.wait()
@@ -250,16 +253,15 @@
     rows = row_factors.shape[0]
     count = block_len // CHUNK
     f32, bf16 = jnp.float32, jnp.bfloat16
-    smem = pl.BlockSpec(memory_space=pltpu.SMEM)
-    hbm = pl.BlockSpec(memory_space=pl.ANY)
+    anywhere = pl.BlockSpec(memory_space=pl.ANY)
     return tuple(pl.pallas_call(
         functools.partial(kernel, strata, groups),
         out_shape=(
             jax.ShapeDtypeStruct((rows, rank), f32),
             jax.ShapeDtypeStruct((block_len, rank), f32),
         ),
-        in_specs=[smem, smem, smem, hbm, hbm, hbm],
-        out_specs=(hbm, hbm),
+        in_specs=[pl.BlockSpec(memory_space=pltpu.HBM)] * 6,
+        out_specs=(anywhere, anywhere),
         scratch_shapes=[
             pltpu.VMEM((rows, rank), f32),
             pltpu.VMEM((block_len, rank), f32),
@@ -278,10 +280,11 @@
             pltpu.VMEM((count, CHUNK + PAD, rank), jnp.int16),
             pltpu.VMEM((HALO, rank), f32),
             pltpu.VMEM((HALO, rank), f32),
-            pltpu.VMEM((HALO, rank), f32),
-            pltpu.VMEM((HALO, rank), f32),
             pltpu.VMEM((4, BAND, BAND + 2 * HALO), bf16),
-            pltpu.SemaphoreType.DMA((3 + count,)),
+            pltpu.SMEM((LAGS,), jnp.int32),
+            pltpu.SMEM((LAGS,), f32),
+            pltpu.SMEM(tile_mask.shape, jnp.int32),
+            pltpu.SemaphoreType.DMA((6 + count,)),
             pltpu.SemaphoreType.DMA((1 + count,)),
             pltpu.SemaphoreType.DMA((2 * count,)),
             pltpu.SemaphoreType.DMA((2 * count,)),
@@ -289,7 +292,7 @@
             pltpu.SemaphoreType.DMA((4,)),
         ],
         compiler_params=pltpu.CompilerParams(
-            collective_id=0, has_side_effects=True, vmem_limit_bytes=48 * 2**20),
+            collective_id=0, has_side_effects=True, vmem_limit_bytes=40 * 2**20),
     )(lags, ar_weights, tile_mask, row_factors, time_factors, values))
 
 

time: 47.5 us -> 49 us (1.032)
  local copies, waits for them, and re-layouts: 6.39 us -> 8.58 us
  Pallas kernels: 40.2 us -> 39.5 us
    unnamed x12 -> x14, local copies, waits for them, and re-layouts: 6.39 us -> 8.58 us
    pallas_call x1, Pallas kernels: 40.2 us -> 39.5 us  [body(): pl.pallas_call(functools.partial(kernel, strata, groups), out_shape=(jax....]
where the time goes in v2:
time: 49 us; the launch traced here: 48.7 us
  Pallas kernels  39.5 us (81%)
  local copies, waits for them, and re-layouts  8.58 us (18%)
  between operations  0.65 us (1%)
    pallas_call x1, Pallas kernels, body(): pl.pallas_call(functools.partial(kernel, strata, groups), out_shape=(jax....  39.5 us
    unnamed x14, local copies, waits for them, and re-layouts  8.58 us

profile of v2, /device:TPU:0, one launch (start us, length us, event | category | flops | bytes accessed | tf_op | source)
XLA Modules:
  0.0 48.7 jit_solution(12565961856558961038)
XLA Ops:
  0.6 0.0 copy-start
  0.6 2.2 %copy-done = bf16[2,1024,1024]{2,1,0:T(8,128)(2,1)S(1)} copy-done((bf16[2,1024,1024]{2,1,0:T(8,128)(2,1)S(1)}, bf16[2,1024,1024]{2,1,0:T(8,128)(2,1)}, u32[]{:S(2)}) %copy-start) | copy-done | bytes 4194328
  2.8 0.0 copy-start.1
  2.8 1.2 %copy-done.1 = f32[1024,256]{1,0:T(8,128)S(1)} copy-done((f32[1024,256]{1,0:T(8,128)S(1)}, f32[1024,256]{1,0:T(8,128)}, u32[]{:S(2)}) %copy-start.1) | copy-done | bytes 1048600
  4.0 0.0 copy-start.2
  4.0 1.2 %copy-done.2 = f32[1024,256]{1,0:T(8,128)S(1)} copy-done((f32[1024,256]{1,0:T(8,128)S(1)}, f32[1024,256]{1,0:T(8,128)}, u32[]{:S(2)}) %copy-start.2) | copy-done | bytes 1048600
  5.3 0.0 copy-start.3
  5.3 0.7 %copy-done.3 = s32[2,8,8]{2,1,0:T(8,128)S(1)} copy-done((s32[2,8,8]{2,1,0:T(8,128)S(1)}, s32[2,8,8]{2,1,0:T(8,128)}, u32[]{:S(2)}) %copy-start.3) | copy-done | bytes 536
  6.0 0.0 copy-start.4
  6.0 0.7 %copy-done.4 = s32[4]{0:T(128)S(1)} copy-done((s32[4]{0:T(128)S(1)}, s32[4]{0:T(128)}, u32[]{:S(2)}) %copy-start.4) | copy-done | bytes 40
  6.6 0.0 copy-start.5
  6.6 0.7 %copy-done.5 = f32[4]{0:T(128)S(1)} copy-done((f32[4]{0:T(128)S(1)}, f32[4]{0:T(128)}, u32[]{:S(2)}) %copy-start.5) | copy-done | bytes 40
  7.3 39.5 %shard_map.77 = (f32[1024,256]{1,0:T(8,128)S(1)}, f32[1024,256]{1,0:T(8,128)S(1)}) custom-call(s32[4]{0:T(128)S(1)} %copy-done.4, f32[4]{0:T(128)S(1)} %copy-done.5, s32[2,8,8]{2,1,0:T(8,128)S(1)} %copy-done.3, f32[1024,256]{1,0:T(8,128)S(1)} %copy-done.1, f32[1024,256]{1,0:T(8,128)S(1)} %copy-done.2, bf16[2,1024,1024]{2,1,0:T(8,128)(2,1)S(1)} %copy-done), custom_call_target="tpu_custom_call" | custom-call | tf_op jit(solution)/shard_map/pallas_call | solution.py:257
  46.7 1.0 %copy.10 = f32[1024,256]{1,0:T(8,128)} copy(f32[1024,256]{1,0:T(8,128)S(1)} %get-tuple-element.4) | data formatting | bytes 2097152
  47.7 1.0 %copy.11 = f32[1024,256]{1,0:T(8,128)} copy(f32[1024,256]{1,0:T(8,128)S(1)} %get-tuple-element.5) | data formatting | bytes 2097152
Async XLA Ops:
  0.6 2.2 %copy-start = (bf16[2,1024,1024]{2,1,0:T(8,128)(2,1)S(1)}, bf16[2,1024,1024]{2,1,0:T(8,128)(2,1)}, u32[]{:S(2)}) copy-start(bf16[2,1024,1024]{2,1,0:T(8,128)(2,1)} %v_hbm.1) | copy-start | bytes 12582916
  2.8 1.2 %copy-start.1 = (f32[1024,256]{1,0:T(8,128)S(1)}, f32[1024,256]{1,0:T(8,128)}, u32[]{:S(2)}) copy-start(f32[1024,256]{1,0:T(8,128)} %f_hbm.1) | copy-start | bytes 3145732
  4.0 1.2 %copy-start.2 = (f32[1024,256]{1,0:T(8,128)S(1)}, f32[1024,256]{1,0:T(8,128)}, u32[]{:S(2)}) copy-start(f32[1024,256]{1,0:T(8,128)} %x_hbm.1) | copy-start | bytes 3145732
  5.3 0.7 %copy-start.3 = (s32[2,8,8]{2,1,0:T(8,128)S(1)}, s32[2,8,8]{2,1,0:T(8,128)}, u32[]{:S(2)}) copy-start(s32[2,8,8]{2,1,0:T(8,128)} %mask_hbm.1) | copy-start | bytes 1540
  6.0 0.7 %copy-start.4 = (s32[4]{0:T(128)S(1)}, s32[4]{0:T(128)}, u32[]{:S(2)}) copy-start(s32[4]{0:T(128)} %lags_hbm.1) | copy-start | bytes 52
  6.6 0.7 %copy-start.5 = (f32[4]{0:T(128)S(1)}, f32[4]{0:T(128)}, u32[]{:S(2)}) copy-start(f32[4]{0:T(128)} %weights_hbm.1) | copy-start | bytes 52

commit v3 on v2

--- a/solution.py
+++ b/solution.py
@@ -10,9 +10,10 @@
 HALO = 64
 LAGS = 4
 TILE = 128
-CHUNK = 256
+CHUNK = 128
 BAND = 128
 PAD = 16
+PARTS = 4
 TOP = 32000.0
 LOG2_E = 1.4426950408889634
 
@@ -77,7 +78,6 @@
     barrier = pltpu.get_barrier_semaphore()
     for peer in (left, right, nxt, prv):
         pl.semaphore_signal(barrier, inc=1, device_id=peer, device_id_type=MESH)
-    pl.semaphore_wait(barrier, 4)
 
     def rim(source, target, at, peer):
         return pltpu.make_async_remote_copy(
@@ -88,8 +88,6 @@
     rim0_l = rim(x_hbm.at[pl.ds(0, HALO)], hi0, 1, left)
     rim1_r = rim(xh1.at[pl.ds(block_len, HALO)], xh1.at[pl.ds(0, HALO)], 2, right)
     rim1_l = rim(xh1.at[pl.ds(HALO, HALO)], xh1.at[pl.ds(HALO + block_len, HALO)], 3, left)
-    rim0_r.start()
-    rim0_l.start()
     forth = {
         j: pltpu.make_async_remote_copy(
             src_ref=xh1.at[inner(j)], dst_ref=xr.at[cols(j)], send_sem=send_sem.at[j],
@@ -202,6 +200,10 @@
         now = ridge_step(x[cols(j), :], xh0, xl0, j) + rate_time * grad
         x1[cols(j), :] = now
         split(now, xh1, xl1, HALO + j * CHUNK, CHUNK)
+        if j == order[0]:
+            pl.semaphore_wait(barrier, 4)
+            rim0_r.start()
+            rim0_l.start()
         forth[j].start()
         if j == order[0]:
             load_v1.start()
@@ -246,6 +248,23 @@
         store.wait()
 
 
+def hand_over(f_in, x_in, f_out, x_out, held, in_sem, out_sem):
+    loads, stores = [], []
+    for at, (source, target) in enumerate(((f_in, f_out), (x_in, x_out))):
+        size = source.shape[0] // PARTS
+        for part in range(PARTS):
+            here = pl.ds(part * size, size)
+            loads.append(pltpu.make_async_copy(source.at[here], held.at[at, here], in_sem.at[at, part]))
+            stores.append(pltpu.make_async_copy(held.at[at, here], target.at[here], out_sem.at[at, part]))
+    for load in loads:
+        load.start()
+    for load, store in zip(loads, stores):
+        load.wait()
+        store.start()
+    for store in stores:
+        store.wait()
+
+
 def body(row_factors, time_factors, values, tile_mask, lags, ar_weights):
     strata = lax.axis_size("stratum")
     groups = lax.axis_size("tm")
@@ -254,7 +273,7 @@
     count = block_len // CHUNK
     f32, bf16 = jnp.float32, jnp.bfloat16
     anywhere = pl.BlockSpec(memory_space=pl.ANY)
-    return tuple(pl.pallas_call(
+    updated = pl.pallas_call(
         functools.partial(kernel, strata, groups),
         out_shape=(
             jax.ShapeDtypeStruct((rows, rank), f32),
@@ -292,8 +311,20 @@
             pltpu.SemaphoreType.DMA((4,)),
         ],
         compiler_params=pltpu.CompilerParams(
-            collective_id=0, has_side_effects=True, vmem_limit_bytes=40 * 2**20),
-    )(lags, ar_weights, tile_mask, row_factors, time_factors, values))
+            collective_id=0, has_side_effects=True, vmem_limit_bytes=60 * 2**20),
+    )(lags, ar_weights, tile_mask, row_factors, time_factors, values)
+    return tuple(pl.pallas_call(
+        hand_over,
+        out_shape=tuple(jax.ShapeDtypeStruct(array.shape, array.dtype) for array in updated),
+        in_specs=[anywhere] * 2,
+        out_specs=(anywhere, anywhere),
+        scratch_shapes=[
+            pltpu.VMEM((2, rows, rank), f32),
+            pltpu.SemaphoreType.DMA((2, PARTS)),
+            pltpu.SemaphoreType.DMA((2, PARTS)),
+        ],
+        compiler_params=pltpu.CompilerParams(vmem_limit_bytes=60 * 2**20),
+    )(*updated))
 
 
 def solution(mesh):

time: 49 us -> 41.9 us (0.86)
  local copies, waits for them, and re-layouts: 8.58 us -> 0 us
  Pallas kernels: 39.5 us -> 41.1 us
    unnamed x14 -> x0, local copies, waits for them, and re-layouts: 8.58 us -> none
    pallas_call x0 -> x1, Pallas kernels: none -> 2.4 us  [body(): pl.pallas_call(hand_over, out_shape=tuple((jax.ShapeDtypeStruct(array.sha...]
    pallas_call x1, Pallas kernels: 39.5 us -> 38.7 us  [body(): pl.pallas_call(functools.partial(kernel, strata, groups), out_shape=(jax....]
where the time goes in v3:
time: 41.9 us; the launch traced here: 41.7 us
  Pallas kernels  41.1 us (98%)
  between operations  0.64 us (2%)
    pallas_call x1, Pallas kernels, body(): pl.pallas_call(functools.partial(kernel, strata, groups), out_shape=(jax....  38.7 us
    pallas_call x1, Pallas kernels, body(): pl.pallas_call(hand_over, out_shape=tuple((jax.ShapeDtypeStruct(array.sha...  2.4 us

profile of v3, /device:TPU:0, one launch (start us, length us, event | category | flops | bytes accessed | tf_op | source)
XLA Modules:
  0.0 41.7 jit_solution(12357657678681306305)
XLA Ops:
  0.6 38.7 %shard_map.77 = (f32[1024,256]{1,0:T(8,128)}, f32[1024,256]{1,0:T(8,128)}) custom-call(s32[4]{0:T(128)} %lags_hbm.1, f32[4]{0:T(128)} %weights_hbm.1, s32[2,8,8]{2,1,0:T(8,128)} %mask_hbm.1, f32[1024,256]{1,0:T(8,128)} %f_hbm.1, f32[1024,256]{1,0:T(8,128)} %x_hbm.1, bf16[2,1024,1024]{2,1,0:T(8,128)(2,1)} %v_hbm.1), custom_call_target="tpu_custom_call" | custom-call | tf_op jit(solution)/shard_map/pallas_call | solution.py:276
  39.3 2.4 %shard_map.78 = (f32[1024,256]{1,0:T(8,128)}, f32[1024,256]{1,0:T(8,128)}) custom-call(f32[1024,256]{1,0:T(8,128)} %get-tuple-element.4.f_in, f32[1024,256]{1,0:T(8,128)} %get-tuple-element.5.x_in), custom_call_target="tpu_custom_call" | custom-call | tf_op jit(solution)/shard_map/pallas_call | solution.py:316
